TPU v7x, 32 devices: a whole 2x2x4 slice. The times are simulated.
32 devices in a mesh: parts: 2 (over x), seq: 16 (over z, y, core).
Axes of the slice: x: 2, y: 2, z: 4, core: 2. Of those that a mesh axis runs over, the one named last changes fastest.
Arguments:
- queries: bfloat16 [4096, 1024], P(('parts', 'seq')), parts along dimension 0, may hold values from -6 to 6
- keys: bfloat16 [4096, 1024], P(('parts', 'seq')), parts along dimension 0, may hold values from -6 to 6
- values: bfloat16 [4096, 1024], P(('parts', 'seq')), parts along dimension 0, may hold values from -6 to 6
- log_forget: float32 [8, 4096], P(None, ('parts', 'seq')), parts along dimension 1, may hold values from -5 to 0
- input_gate: float32 [8, 4096], P(None, ('parts', 'seq')), parts along dimension 1, may hold values from 0.1 to 1
- ridge: float32 [8], replicated, may hold values from 0.25 to 4
- gain: float32 [1024], replicated, may hold values from 0.25 to 1.75
- out_weight: bfloat16 [1024, 2048], P('seq'), may hold values from -0.1875 to 0.1875
Outputs:
- mixed: bfloat16 [4096, 2048], P(('parts', 'seq')), parts along dimension 0
There are 2 independent parts, one for each index of `parts`. A program takes and returns all parts, laid end to end along the dimension named above; an argument that names none is the same for every part. Nothing has to cross between parts.
All inputs are finite; a program needn't handle non-finite values. Where the computation divides by a largest or mean magnitude, that divisor is 1e-20 or more.
Results may differ from a plain program's by a relative error of at most 0.007.
Values may be sent and summed in bfloat16 or wider, within the bound.
No kernel may reach another device: no remote copies, remote signals or barrier semaphores. Data moves between devices by JAX's collectives and lax.ppermute only.
A program may use at most 192 MiB of HBM per device.

v0:
```python
import jax
import jax.numpy as jnp
from jax import lax
from jax.sharding import PartitionSpec as P

HEADS = 8
DH = 128
C = 128
NEWTON = 6
CORR = 4
highest = lax.Precision.HIGHEST


def carried_in(array, axis, join, neutral):
    place = lax.axis_index(axis)
    gathered = jax.tree.map(
        lambda a, kind: lax.all_gather(a.astype(kind), axis), array, (jnp.bfloat16, jnp.bfloat16)
    )
    state = jax.tree.map(lambda a, e: jnp.zeros_like(a) + jnp.asarray(e, a.dtype), array, neutral)

    def one(step, state):
        return join(
            state,
            jax.tree.map(
                lambda a, own: lax.dynamic_index_in_dim(a, step, 0, False).astype(own.dtype),
                gathered,
                array,
            ),
        )

    return lax.fori_loop(0, place, one, state)


def prefix(value, axis, join, neutral):
    count, mine = (lax.axis_size(axis), lax.axis_index(axis))
    pieces = jax.tree.map(lambda part: lax.all_gather(part, axis), value)
    total = jax.tree.map(
        lambda part, zero: jnp.full_like(part, 0) + jnp.asarray(zero, part.dtype), value, neutral
    )

    def step(position, total):
        longer = join(total, jax.tree.map(lambda part: part[position], pieces))
        return jax.tree.map(lambda new, old: jnp.where(position < mine, new, old), longer, total)

    return lax.fori_loop(0, count - 1, step, total)


def product(left, right):
    return jnp.matmul(left, right, precision=highest)


def unit_rows(field):
    return field * lax.rsqrt(jnp.sum(field * field, axis=-1, keepdims=True) + 1e-06)


def add_pairs(earlier, later):
    shrink = jnp.exp(later[0])[:, None, None]
    return (earlier[0] + later[0], shrink * earlier[1] + later[1])


def newton_inverse(system):
    bound = jnp.max(jnp.sum(jnp.abs(system), axis=-1), axis=-1)
    identity = jnp.eye(system.shape[-1], dtype=system.dtype)
    approx = identity / bound[..., None, None]
    for iteration in range(NEWTON):
        approx = product(approx, 2.0 * identity - product(system, approx))
    return approx


def solve_blocks(query_rows, key_t, beta_keys, start_gram, pre_gram, decay_row, mixing, ridge_col):
    identity = jnp.eye(query_rows.shape[-1], dtype=query_rows.dtype)
    system = start_gram + pre_gram + ridge_col * identity
    inverse = newton_inverse(system)
    solved = product(query_rows, inverse)
    for iteration in range(CORR - 1):
        attention_scores = mixing * product(solved, key_t)
        applied = (
            decay_row * product(solved, start_gram)
            + product(attention_scores, beta_keys)
            + ridge_col * solved
        )
        solved = solved + product(query_rows - applied, inverse)
    attention_scores = mixing * product(solved, key_t)
    return (solved, attention_scores)


def shift_down(field):
    return jnp.concatenate([jnp.zeros_like(field), field[:-1]], axis=0)


def on_device(queries, keys, values, log_forget, input_gate, ridge, gain, out_weight):
    tokens = queries.shape[0]
    count = tokens // C

    def blocks(field):
        return field.astype(jnp.float32).reshape(count, C, HEADS, DH).transpose(0, 2, 1, 3)

    def gate_blocks(field):
        return field.reshape(HEADS, count, C).transpose(1, 0, 2)

    query_all = unit_rows(blocks(queries))
    key_all = unit_rows(blocks(keys))
    value_all = blocks(values)
    forget_all = gate_blocks(log_forget)
    beta_all = gate_blocks(input_gate)
    running = jnp.cumsum(forget_all, axis=-1)
    block_decay = running[..., -1]
    decay_row = jnp.exp(running)[..., None]
    lower_mask = jnp.tril(jnp.ones((C, C), jnp.float32))
    mixing = lower_mask * jnp.exp(jnp.minimum(running[..., :, None] - running[..., None, :], 0.0))
    tail = (jnp.exp(block_decay[..., None] - running) * beta_all)[..., None]
    beta_col = beta_all[..., None]
    beta_keys = beta_col * key_all
    beta_values = beta_col * value_all
    key_t = jnp.swapaxes(key_all, -1, -2)
    block_grams = product(key_t, tail * key_all)
    block_states = product(key_t, tail * value_all)
    pre_grams = product(key_t, beta_keys)
    level_incl = jnp.cumsum(block_decay, axis=0)
    level_exclusive = level_incl - block_decay
    block_mask = jnp.tril(jnp.ones((count, count), jnp.float32))
    carry_weights = block_mask[:, :, None] * jnp.exp(
        jnp.minimum(level_incl[:, None, :] - level_incl[None, :, :], 0.0)
    )
    gram_incl = jnp.einsum("bch,chij->bhij", carry_weights, block_grams, precision=highest)
    state_incl = jnp.einsum("bch,chij->bhij", carry_weights, block_states, precision=highest)
    gram_local = shift_down(gram_incl)
    state_local = shift_down(state_incl)
    section_decay = level_incl[-1]
    gram_total = gram_incl[-1]
    state_total = state_incl[-1]
    carried = jnp.exp(level_exclusive)[..., None, None]
    ridge_col = ridge[None, :, None, None]
    zeros = jnp.zeros((HEADS, DH, DH), jnp.float32)
    zero_levels = jnp.zeros((HEADS,), jnp.float32)
    decay_before, gram_before = carried_in(
        (section_decay, gram_total), "seq", add_pairs, (zero_levels, zeros)
    )
    start_gram = carried * gram_before[None] + gram_local
    solved, attention_scores = solve_blocks(
        query_all, key_t, beta_keys, start_gram, pre_grams, decay_row, mixing, ridge_col
    )
    decay_again, state_before = prefix(
        (section_decay, state_total), "seq", add_pairs, (zero_levels, zeros)
    )
    start_state = carried * state_before[None] + state_local
    outputs = decay_row * product(solved, start_state) + product(attention_scores, beta_values)
    normed = outputs * lax.rsqrt(jnp.mean(outputs * outputs, axis=-1, keepdims=True) + 1e-06)
    normed = normed.transpose(0, 2, 1, 3).reshape(tokens, HEADS * DH) * gain
    normed = normed.astype(jnp.bfloat16)
    mixed = jnp.dot(
        normed,
        lax.all_gather(out_weight, "seq", axis=0, tiled=True),
        preferred_element_type=jnp.float32,
    )
    return mixed.astype(jnp.bfloat16)


def solution(mesh):
    placed = (
        P(("parts", "seq"), None),
        P(("parts", "seq"), None),
        P(("parts", "seq"), None),
        P(None, ("parts", "seq")),
        P(None, ("parts", "seq")),
        P(),
        P(),
        P("seq", None),
    )
    return jax.shard_map(
        on_device, mesh=mesh, in_specs=placed, out_specs=P(("parts", "seq"), None), check_vma=False
    )
```

profile of v0, /device:TPU:0, one launch (start us, length us, event | category | flops | bytes accessed | tf_op | source)
XLA Modules:
  0.0 202.5 jit_solution(14111731885373058151)
XLA Ops:
  10.8 1.9 fusion.14
  12.9 2.0 convolution_multiply_fusion.2
  15.7 23.1 %all-gather.1 = f32[16,8,1]{1,2,0:T(1,128)S(1)} all-gather(f32[1,8,1]{1,2,0:T(1,128)S(1)} %copy.278), channel_id=3, replica_groups=mesh['parts'=2,'seq'=16] {'seq'}, dimensions={0}, use_global_device_ids=true | all-gather | bytes 544 | tf_op jit(solution)/shard_map/all_gather | solution.py:36
  38.9 17.7 %all-gather.3 = bf16[16,8,1]{1,2,0:T(2,128)(2,1)S(1)} all-gather(bf16[1,8,1]{1,2,0:T(2,128)(2,1)S(1)} %convert_element_type.59), channel_id=5, replica_groups=mesh['parts'=2,'seq'=16] {'seq'}, dimensions={0}, use_global_device_ids=true | all-gather | bytes 272 | tf_op jit(solution)/shard_map/all_gather | solution.py:17
  56.9 9.2 %all-gather.10.cloned.1.call-done = bf16[128,128,128]{2,1,0:T(8,128)(2,1)} async-done(((bf16[8,128,128]{2,1,0:T(8,128)(2,1)}), bf16[128,128,128]{2,1,0:T(8,128)(2,1)}) %all-gather.10.cloned.1.call-update) | async-done | bytes 4194320 | tf_op jit(solution)/shard_map/all_gather | solution.py:17
  66.5 1.2 abs_reduce_fusion
  67.9 1.3 convolution_subtract_fusion.5
  78.9 1.2 fusion.30
  81.1 1.3 convolution_multiply_fusion.8
  83.1 2.2 %fusion.9 = f32[8,128,128]{1,2,0:T(8,128)S(1)} fusion(f32[8,128,128]{1,2,0:T(8,128)S(1)} %convolution_multiply_fusion.8, f32[8,128,128]{2,1,0:T(8,128)S(1)} %convolution_multiply_fusion.7, f32[8,128,128]{1,2,0:T(8,128)} %copy.214, f32[1,8,128,128]{2,3,1,0:T(8,128)S(1)} %bitcast.176, f32[1,8,128,128]{2,3,1,0:T(8,128)S(1)} %bitcast.168, f32[8]{0:T(128)S(1)} %copy-done.5, ...), kind=kOutput, calls=%fused_computation.38 | convolution fusion | flops 202244096 | bytes 3158048 | tf_op jit(solution)/shard_map/dot_general | solution.py:49
  88.1 1.2 fusion.11
  92.1 1.2 fusion.13
  94.3 1.3 convolution_multiply_fusion
  95.7 45.4 %all-gather.12.cloned.1.call-done = f32[128,128,128]{2,1,0:T(8,128)} async-done(((f32[8,128,128]{2,1,0:T(8,128)}), f32[128,128,128]{2,1,0:T(8,128)}) %all-gather.12.cloned.1.call-update) | async-done | bytes 8388624 | tf_op jit(solution)/shard_map/all_gather | solution.py:36
  141.1 18.3 %while.27 = (s32[]{:T(128)}, f32[8,128,128]{2,1,0:T(8,128)S(1)}, s32[]{:T(128)}, f32[16,8]{1,0:T(8,128)S(1)}, f32[16,8,128,128]{3,2,1,0:T(8,128)}, /*index=5*/s32[]{:T(128)}, s32[]{:T(128)}) while((s32[]{:T(128)}, f32[8,128,128]{2,1,0:T(8,128)S(1)}, s32[]{:T(128)}, f32[16,8]{1,0:T(8,128)S(1)}, f32[16,8,128,128]{3,2,1,0:T(8,128)}, ...), condition=%wide.region_8.9_spmd.clone, body=%wide.region_7.8_spmd.clone.sunk | while | flops 524292 | bytes 1573065 | solution.py:45
  141.1 1.2 fusion.131
  143.6 1.2 fusion.131
  144.8 1.2 fusion.131
  148.4 1.2 fusion.131
  149.7 1.2 fusion.131
  155.8 1.2 fusion.131
  160.3 1.2 multiply_reduce_fusion
  161.7 30.5 %all-gather.8.cloned.1.call-done = bf16[1024,2048]{1,0:T(8,128)(2,1)} async-done(((bf16[64,2048]{1,0:T(8,128)(2,1)}), bf16[1024,2048]{1,0:T(8,128)(2,1)}) %all-gather.8.cloned.1.call-update) | async-done | bytes 4194320 | tf_op jit(solution)/shard_map/all_gather | solution.py:153
  192.2 3.7 %convolution_convert_fusion = bf16[128,2048]{1,0:T(8,128)(2,1)} fusion(bf16[128,1024]{0,1:T(8,128)(2,1)S(1)} %fusion.15, bf16[1024,2048]{1,0:T(8,128)(2,1)} %all-gather.8.cloned.1.call-done), kind=kOutput, calls=%fused_computation.5 | convolution fusion | flops 537133056 | bytes 4980736 | tf_op jit(solution)/shard_map/dot_general | solution.py:151
  (92 shorter events, 35.5 us)
Async XLA Ops:
  6.5 6.2 %copy-start.3 = (bf16[128,1024]{1,0:T(8,128)(2,1)S(1)}, bf16[128,1024]{1,0:T(8,128)(2,1)}, u32[]{:S(2)}) copy-start(bf16[128,1024]{1,0:T(8,128)(2,1)} %param.14) | copy-start | bytes 786436
  6.5 59.5 %all-gather.10.cloned.1.call-start = ((), (), s32[]{:S(2)}) async-start(), calls=%async_computation.1 | async-start | bytes 4456448 | tf_op jit(solution)/shard_map/all_gather | solution.py:17
  12.7 128.4 %all-gather.12.cloned.1.call-start = ((), (), s32[]{:S(2)}) async-start(), calls=%async_computation.2 | async-start | bytes 8912896 | tf_op jit(solution)/shard_map/all_gather | solution.py:36
  12.9 53.1 %copy-start = (f32[128,1024]{0,1:T(8,128)}, f32[128,1024]{0,1:T(8,128)S(1)}, u32[]{:S(2)}) copy-start(f32[128,1024]{0,1:T(8,128)S(1)} %copy.276) | copy-start | bytes 1572868
  14.9 177.3 %all-gather.8.cloned.1.call-start = ((), (), s32[]{:S(2)}) async-start(), calls=%async_computation | async-start | bytes 4456448 | tf_op jit(solution)/shard_map/all_gather | solution.py:153
  56.8 9.7 %copy-start.4 = (f32[8,128]{1,0:T(8,128)S(1)}, f32[8,128]{1,0:T(8,128)}, u32[]{:S(2)}) copy-start(f32[8,128]{1,0:T(8,128)} %param.16) | copy-start | bytes 12292
  56.8 9.7 %copy-start.5 = (f32[8]{0:T(128)S(1)}, f32[8]{0:T(128)}, u32[]{:S(2)}) copy-start(f32[8]{0:T(128)} %param.17) | copy-start | bytes 100
  81.1 4.2 %copy-start.2 = (f32[8,128,128]{1,2,0:T(8,128)S(1)}, f32[8,128,128]{1,2,0:T(8,128)}, u32[]{:S(2)}) copy-start(f32[8,128,128]{1,2,0:T(8,128)} %copy.214) | copy-start | bytes 1572868
  141.1 19.2 %copy-start.1 = (f32[128,1024]{0,1:T(8,128)S(1)}, f32[128,1024]{0,1:T(8,128)}, u32[]{:S(2)}) copy-start(f32[128,1024]{0,1:T(8,128)} %copy-done) | copy-start | bytes 1572868
  159.4 2.2 %copy-start.6 = (f32[1024]{0:T(1024)S(1)}, f32[1024]{0:T(1024)}, u32[]{:S(2)}) copy-start(f32[1024]{0:T(1024)} %param.18) | copy-start | bytes 12292
Sparse Core Ops, SparseCore 0:
  12.8 53.1 all-gather.9
  68.2 72.8 all-gather.11
  143.2 48.9 all-gather.7
where the time goes:
time: 204 us; the launch traced here: 202 us
  waiting for transfers between devices  85.8 us (42%)
  blocking collectives  40.9 us (20%)
  matrix products  37.4 us (18%)
  other arithmetic  19.9 us (10%)
  between operations  13.5 us (7%)
  local copies, waits for them, and re-layouts  4.31 us (2%)
    all_gather x1, waiting for transfers between devices, prefix(): pieces = jax.tree.map(lambda part: lax.all_gather(part, axis), value)  45.4 us
    dot_general x31, matrix products, product(): return jnp.matmul(left, right, precision=highest)  33.7 us
    all_gather x1, waiting for transfers between devices, on_device(): lax.all_gather(out_weight, 'seq', axis=0, tiled=True)  30.5 us
    all_gather x1, blocking collectives, prefix(): pieces = jax.tree.map(lambda part: lax.all_gather(part, axis), value)  23.1 us
    all_gather x1, blocking collectives, carried_in(): lax.all_gather(a.astype(kind), axis)  17.7 us
    select_n x15, other arithmetic, step(): jnp.where(position < mine, new, old)  17.7 us
    all_gather x1, waiting for transfers between devices, carried_in(): lax.all_gather(a.astype(kind), axis)  9.19 us
  transfers between devices with their start and end apart: 3, of which 3 were waited for; matrix products, arithmetic and copies ran while one was open for 26% of the time, Pallas kernels for 0%

commit v1 on v0

--- a/solution.py
+++ b/solution.py
@@ -9,6 +9,22 @@
 NEWTON = 6
 CORR = 4
 highest = lax.Precision.HIGHEST
+
+
+def gather_around(x, axis, dim):
+    ways, here, step = (lax.axis_size(axis), lax.axis_index(axis), x.shape[dim])
+    dims = [n * ways if d == dim else n for d, n in enumerate(x.shape)]
+    full = lax.dynamic_update_slice_in_dim(jnp.zeros(dims, x.dtype), x, here * step, axis=dim)
+    going_up = going_down = x
+    for far in range(1, ways // 2 + 1):
+        going_up = lax.ppermute(going_up, axis, [(d, (d + 1) % ways) for d in range(ways)])
+        full = lax.dynamic_update_slice_in_dim(full, going_up, (here - far) % ways * step, axis=dim)
+        if 2 * far < ways:
+            going_down = lax.ppermute(going_down, axis, [(d, (d - 1) % ways) for d in range(ways)])
+            full = lax.dynamic_update_slice_in_dim(
+                full, going_down, (here + far) % ways * step, axis=dim
+            )
+    return full
 
 
 def carried_in(array, axis, join, neutral):
@@ -148,11 +164,7 @@
     normed = outputs * lax.rsqrt(jnp.mean(outputs * outputs, axis=-1, keepdims=True) + 1e-06)
     normed = normed.transpose(0, 2, 1, 3).reshape(tokens, HEADS * DH) * gain
     normed = normed.astype(jnp.bfloat16)
-    mixed = jnp.dot(
-        normed,
-        lax.all_gather(out_weight, "seq", axis=0, tiled=True),
-        preferred_element_type=jnp.float32,
-    )
+    mixed = jnp.dot(normed, gather_around(out_weight, "seq", 0), preferred_element_type=jnp.float32)
     return mixed.astype(jnp.bfloat16)
 
 

time: 204 us -> 216 us (1.059)
  the two profiles are of different devices: /device:TPU:0 before, /device:TPU:31 now
where the time goes in v1:
time: 216 us; the launch traced here: 214 us
  blocking collectives  38.8 us (18%)
  matrix products  37.6 us (17%)
  other arithmetic  36.8 us (17%)
  starting transfers between devices  34.1 us (16%)
  waiting for transfers between devices  33.2 us (15%)
  local copies, waits for them, and re-layouts  18.4 us (9%)
  between operations  14.2 us (7%)
    dot_general x31, matrix products, product(): return jnp.matmul(left, right, precision=highest)  33.9 us
    ppermute x8, starting transfers between devices, gather_around(): lax.ppermute(going_up, axis, [(d, (d + 1) % ways) for d in range(ways)])  33.8 us
    ppermute x7, waiting for transfers between devices, gather_around(): lax.ppermute(going_down, axis, [(d, (d - 1) % ways) for d in range(ways)])  22 us
    all_gather x1, blocking collectives, prefix(): pieces = jax.tree.map(lambda part: lax.all_gather(part, axis), value)  19.9 us
    all_gather x1, blocking collectives, carried_in(): lax.all_gather(a.astype(kind), axis)  18.8 us
    select_n x15, other arithmetic, step(): jnp.where(position < mine, new, old)  17.6 us
    add x15, other arithmetic, add_pairs(): return (earlier[0] + later[0], shrink * earlier[1] + later[1])  16.7 us
    ppermute x8, waiting for transfers between devices, gather_around(): lax.ppermute(going_up, axis, [(d, (d + 1) % ways) for d in range(ways)])  11.2 us
  transfers between devices with their start and end apart: 17, of which 10 were waited for; matrix products, arithmetic and copies ran while one was open for 29% of the time, Pallas kernels for 0%

profile of v1, /device:TPU:31, one launch (start us, length us, event | category | flops | bytes accessed | tf_op | source)
XLA Modules:
  0.0 214.2 jit_solution(13944910420782793269)
XLA Ops:
  10.8 1.9 fusion.14
  12.9 2.0 convolution_multiply_fusion.2
  16.1 18.8 %all-gather.3 = bf16[16,8,1]{1,2,0:T(2,128)(2,1)S(1)} all-gather(bf16[1,8,1]{1,2,0:T(2,128)(2,1)S(1)} %convert_element_type.59), channel_id=5, replica_groups=mesh['parts'=2,'seq'=16] {'seq'}, dimensions={0}, use_global_device_ids=true | all-gather | bytes 272 | tf_op jit(solution)/shard_map/all_gather | solution.py:33
  35.2 19.9 %all-gather.1 = f32[16,8,1]{1,2,0:T(1,128)S(1)} all-gather(f32[1,8,1]{1,2,0:T(1,128)S(1)} %copy.278), channel_id=3, replica_groups=mesh['parts'=2,'seq'=16] {'seq'}, dimensions={0}, use_global_device_ids=true | all-gather | bytes 544 | tf_op jit(solution)/shard_map/all_gather | solution.py:52
  55.2 2.5 %broadcast_in_dim.13 = bf16[1024,2048]{1,0:T(8,128)(2,1)} broadcast(bf16[]{:T(256)} %constant.156.clone.1), dimensions={} | broadcast | bytes 4194306 | tf_op jit(solution)/shard_map/broadcast_in_dim | solution.py:17
  58.3 2.8 %collective-permute-start.2 = (bf16[64,2048]{1,0:T(8,128)(2,1)S(1)}, bf16[64,2048]{1,0:T(8,128)(2,1)S(1)}, u32[]{:S(2)}, u32[]{:S(2)}) collective-permute-start(bf16[64,2048]{1,0:T(8,128)(2,1)S(1)} %collective-permute-done), channel_id=1, source_target_pairs={{0,1},{1,2},{2,3},{3,4},{4,5},{5,6},{6,7},{7,8},{8,9},{9,10},{10,1... | collective-permute-start | bytes 786440 | tf_op jit(solution)/shard_map/ppermute | solution.py:20
  64.4 5.3 %collective-permute-start.4 = (bf16[64,2048]{1,0:T(8,128)(2,1)S(1)}, bf16[64,2048]{1,0:T(8,128)(2,1)S(1)}, u32[]{:S(2)}, u32[]{:S(2)}) collective-permute-start(bf16[64,2048]{1,0:T(8,128)(2,1)S(1)} %collective-permute-done.2), channel_id=1, source_target_pairs={{0,1},{1,2},{2,3},{3,4},{4,5},{5,6},{6,7},{7,8},{8,9},{9,10},{10,1... | collective-permute-start | bytes 786440 | tf_op jit(solution)/shard_map/ppermute | solution.py:20
  71.2 1.9 collective-permute-done.4
  73.0 5.3 %collective-permute-start.6 = (bf16[64,2048]{1,0:T(8,128)(2,1)S(1)}, bf16[64,2048]{1,0:T(8,128)(2,1)S(1)}, u32[]{:S(2)}, u32[]{:S(2)}) collective-permute-start(bf16[64,2048]{1,0:T(8,128)(2,1)S(1)} %collective-permute-done.4), channel_id=1, source_target_pairs={{0,1},{1,2},{2,3},{3,4},{4,5},{5,6},{6,7},{7,8},{8,9},{9,10},{10,1... | collective-permute-start | bytes 786440 | tf_op jit(solution)/shard_map/ppermute | solution.py:20
  78.3 5.3 %collective-permute-done.5 = bf16[64,2048]{1,0:T(8,128)(2,1)S(1)} collective-permute-done((bf16[64,2048]{1,0:T(8,128)(2,1)S(1)}, bf16[64,2048]{1,0:T(8,128)(2,1)S(1)}, u32[]{:S(2)}, u32[]{:S(2)}) %collective-permute-start.5) | collective-permute-done | bytes 262176 | tf_op jit(solution)/shard_map/ppermute | solution.py:23
  86.8 5.1 %collective-permute-start.8 = (bf16[64,2048]{1,0:T(8,128)(2,1)S(1)}, bf16[64,2048]{1,0:T(8,128)(2,1)S(1)}, u32[]{:S(2)}, u32[]{:S(2)}) collective-permute-start(bf16[64,2048]{1,0:T(8,128)(2,1)S(1)} %collective-permute-done.6), channel_id=1, source_target_pairs={{0,1},{1,2},{2,3},{3,4},{4,5},{5,6},{6,7},{7,8},{8,9},{9,10},{10,1... | collective-permute-start | bytes 786440 | tf_op jit(solution)/shard_map/ppermute | solution.py:20
  91.9 5.5 %collective-permute-done.7 = bf16[64,2048]{1,0:T(8,128)(2,1)S(1)} collective-permute-done((bf16[64,2048]{1,0:T(8,128)(2,1)S(1)}, bf16[64,2048]{1,0:T(8,128)(2,1)S(1)}, u32[]{:S(2)}, u32[]{:S(2)}) %collective-permute-start.7) | collective-permute-done | bytes 262176 | tf_op jit(solution)/shard_map/ppermute | solution.py:23
  98.9 4.4 %collective-permute-start.10 = (bf16[64,2048]{1,0:T(8,128)(2,1)S(1)}, bf16[64,2048]{1,0:T(8,128)(2,1)S(1)}, u32[]{:S(2)}, u32[]{:S(2)}) collective-permute-start(bf16[64,2048]{1,0:T(8,128)(2,1)S(1)} %collective-permute-done.8), channel_id=1, source_target_pairs={{0,1},{1,2},{2,3},{3,4},{4,5},{5,6},{6,7},{7,8},{8,9},{9,10},{10,1... | collective-permute-start | bytes 786440 | tf_op jit(solution)/shard_map/ppermute | solution.py:20
  103.3 5.4 %collective-permute-done.9 = bf16[64,2048]{1,0:T(8,128)(2,1)S(1)} collective-permute-done((bf16[64,2048]{1,0:T(8,128)(2,1)S(1)}, bf16[64,2048]{1,0:T(8,128)(2,1)S(1)}, u32[]{:S(2)}, u32[]{:S(2)}) %collective-permute-start.9) | collective-permute-done | bytes 262176 | tf_op jit(solution)/shard_map/ppermute | solution.py:23
  110.2 2.0 collective-permute-done.10
  112.2 5.2 %collective-permute-start.12 = (bf16[64,2048]{1,0:T(8,128)(2,1)S(1)}, bf16[64,2048]{1,0:T(8,128)(2,1)S(1)}, u32[]{:S(2)}, u32[]{:S(2)}) collective-permute-start(bf16[64,2048]{1,0:T(8,128)(2,1)S(1)} %collective-permute-done.10), channel_id=1, source_target_pairs={{0,1},{1,2},{2,3},{3,4},{4,5},{5,6},{6,7},{7,8},{8,9},{9,10},{10,1... | collective-permute-start | bytes 786440 | tf_op jit(solution)/shard_map/ppermute | solution.py:20
  117.4 5.7 %collective-permute-done.11 = bf16[64,2048]{1,0:T(8,128)(2,1)S(1)} collective-permute-done((bf16[64,2048]{1,0:T(8,128)(2,1)S(1)}, bf16[64,2048]{1,0:T(8,128)(2,1)S(1)}, u32[]{:S(2)}, u32[]{:S(2)}) %collective-permute-start.11) | collective-permute-done | bytes 262176 | tf_op jit(solution)/shard_map/ppermute | solution.py:23
  124.5 2.0 collective-permute-done.12
  126.5 5.2 %collective-permute-start.14 = (bf16[64,2048]{1,0:T(8,128)(2,1)S(1)}, bf16[64,2048]{1,0:T(8,128)(2,1)S(1)}, u32[]{:S(2)}, u32[]{:S(2)}) collective-permute-start(bf16[64,2048]{1,0:T(8,128)(2,1)S(1)} %collective-permute-done.12), channel_id=1, source_target_pairs={{0,1},{1,2},{2,3},{3,4},{4,5},{5,6},{6,7},{7,8},{8,9},{9,10},{10,1... | collective-permute-start | bytes 786440 | tf_op jit(solution)/shard_map/ppermute | solution.py:20
  133.1 1.9 collective-permute-done.14
  135.7 17.5 %while.26 = (s32[]{:T(128)}, f32[8,128,128]{2,1,0:T(8,128)S(1)}, s32[]{:T(128)}, bf16[16,8]{1,0:T(8,128)(2,1)S(1)}, bf16[16,8,128,128]{3,2,1,0:T(8,128)(2,1)}, /*index=5*/s32[]{:T(128)}, s32[]{:T(128)}, s32[]{:T(128)}) while((s32[]{:T(128)}, f32[8,128,128]{2,1,0:T(8,128)S(1)}, s32[]{:T(128)}, bf16[16,8]{1,0:T(8,128)(2,1)S(1)}, ...), condition=%wide.region_4.5_spmd, body=%wide.region_3.4_spmd.sunk | while | flops 393229 | bytes 1310935 | solution.py:47
  170.1 2.3 %fusion.9 = f32[8,128,128]{1,2,0:T(8,128)S(1)} fusion(f32[8,128,128]{1,2,0:T(8,128)S(1)} %convolution_multiply_fusion.8, f32[8,128,128]{2,1,0:T(8,128)S(1)} %convolution_multiply_fusion.7, f32[8,128,128]{1,2,0:T(8,128)} %copy.214, f32[1,8,128,128]{2,3,1,0:T(8,128)S(1)} %bitcast.176, f32[1,8,128,128]{2,3,1,0:T(8,128)S(1)} %bitcast.168, f32[8]{0:T(128)S(1)} %copy-done.6, ...), kind=kOutput, calls=%fused_computation.38 | convolution fusion | flops 202244096 | bytes 3158048 | tf_op jit(solution)/shard_map/dot_general | solution.py:65
  182.9 18.3 %while.27 = (s32[]{:T(128)}, f32[8,128,128]{2,1,0:T(8,128)S(1)}, s32[]{:T(128)}, f32[16,8]{1,0:T(8,128)S(1)}, f32[16,8,128,128]{3,2,1,0:T(8,128)}, /*index=5*/s32[]{:T(128)}, s32[]{:T(128)}) while((s32[]{:T(128)}, f32[8,128,128]{2,1,0:T(8,128)S(1)}, s32[]{:T(128)}, f32[16,8]{1,0:T(8,128)S(1)}, f32[16,8,128,128]{3,2,1,0:T(8,128)}, ...), condition=%wide.region_8.9_spmd.clone, body=%wide.region_7.8_spmd.clone.sunk | while | flops 524292 | bytes 1573073 | solution.py:61
  203.6 3.7 %convolution_convert_fusion = bf16[128,2048]{1,0:T(8,128)(2,1)} fusion(bf16[128,1024]{0,1:T(8,128)(2,1)S(1)} %fusion.15, bf16[1024,2048]{1,0:T(8,128)(2,1)} %constant_dynamic-update-slice_fusion), kind=kOutput, calls=%fused_computation.5 | convolution fusion | flops 537133056 | bytes 4980736 | tf_op jit(solution)/shard_map/dot_general | solution.py:167
  (168 shorter events, 84.8 us)
Async XLA Ops:
  6.5 6.2 %copy-start.3 = (bf16[128,1024]{1,0:T(8,128)(2,1)S(1)}, bf16[128,1024]{1,0:T(8,128)(2,1)}, u32[]{:S(2)}) copy-start(bf16[128,1024]{1,0:T(8,128)(2,1)} %param.14) | copy-start | bytes 786436
  6.5 8.4 %copy-start.4 = (bf16[64,2048]{1,0:T(8,128)(2,1)S(1)}, bf16[64,2048]{1,0:T(8,128)(2,1)}, u32[]{:S(2)}) copy-start(bf16[64,2048]{1,0:T(8,128)(2,1)} %param.19) | copy-start | bytes 786436
  6.5 129.1 %all-gather.7.cloned.1.call-start = ((), (), s32[]{:S(2)}) async-start(), calls=%async_computation | async-start | bytes 4456448 | tf_op jit(solution)/shard_map/all_gather | solution.py:33
  12.7 170.2 %all-gather.9.cloned.1.call-start = ((), (), s32[]{:S(2)}) async-start(), calls=%async_computation.1 | async-start | bytes 8912896 | tf_op jit(solution)/shard_map/all_gather | solution.py:52
  12.9 49.7 %copy-start = (f32[128,1024]{0,1:T(8,128)}, f32[128,1024]{0,1:T(8,128)S(1)}, u32[]{:S(2)}) copy-start(f32[128,1024]{0,1:T(8,128)S(1)} %copy.276) | copy-start | bytes 1572868
  15.0 43.3 %collective-permute-start = (bf16[64,2048]{1,0:T(8,128)(2,1)S(1)}, bf16[64,2048]{1,0:T(8,128)(2,1)S(1)}, u32[]{:S(2)}, u32[]{:S(2)}) collective-permute-start(bf16[64,2048]{1,0:T(8,128)(2,1)S(1)} %copy-done.4), channel_id=1, source_target_pairs={{0,1},{1,2},{2,3},{3,4},{4,5},{5,6},{6,7},{7,8},{8,9},{9,10},{10,1... | collective-permute-start | bytes 786440 | tf_op jit(solution)/shard_map/ppermute | solution.py:20
  15.5 45.6 %collective-permute-start.1 = (bf16[64,2048]{1,0:T(8,128)(2,1)S(1)}, bf16[64,2048]{1,0:T(8,128)(2,1)S(1)}, u32[]{:S(2)}, u32[]{:S(2)}) collective-permute-start(bf16[64,2048]{1,0:T(8,128)(2,1)S(1)} %copy-done.4), channel_id=1, source_target_pairs={{0,15},{1,0},{2,1},{3,2},{4,3},{5,4},{6,5},{7,6},{8,7},{9,8},{10,9... | collective-permute-start | bytes 786440 | tf_op jit(solution)/shard_map/ppermute | solution.py:23
  58.3 6.1 %collective-permute-start.2 = (bf16[64,2048]{1,0:T(8,128)(2,1)S(1)}, bf16[64,2048]{1,0:T(8,128)(2,1)S(1)}, u32[]{:S(2)}, u32[]{:S(2)}) collective-permute-start(bf16[64,2048]{1,0:T(8,128)(2,1)S(1)} %collective-permute-done), channel_id=1, source_target_pairs={{0,1},{1,2},{2,3},{3,4},{4,5},{5,6},{6,7},{7,8},{8,9},{9,10},{10,1... | collective-permute-start | bytes 786440 | tf_op jit(solution)/shard_map/ppermute | solution.py:20
  61.1 8.6 %collective-permute-start.3 = (bf16[64,2048]{1,0:T(8,128)(2,1)S(1)}, bf16[64,2048]{1,0:T(8,128)(2,1)S(1)}, u32[]{:S(2)}, u32[]{:S(2)}) collective-permute-start(bf16[64,2048]{1,0:T(8,128)(2,1)S(1)} %collective-permute-done.1), channel_id=1, source_target_pairs={{0,15},{1,0},{2,1},{3,2},{4,3},{5,4},{6,5},{7,6},{8,7},{9,8},{10,9... | collective-permute-start | bytes 786440 | tf_op jit(solution)/shard_map/ppermute | solution.py:23
  64.4 8.6 %collective-permute-start.4 = (bf16[64,2048]{1,0:T(8,128)(2,1)S(1)}, bf16[64,2048]{1,0:T(8,128)(2,1)S(1)}, u32[]{:S(2)}, u32[]{:S(2)}) collective-permute-start(bf16[64,2048]{1,0:T(8,128)(2,1)S(1)} %collective-permute-done.2), channel_id=1, source_target_pairs={{0,1},{1,2},{2,3},{3,4},{4,5},{5,6},{6,7},{7,8},{8,9},{9,10},{10,1... | collective-permute-start | bytes 786440 | tf_op jit(solution)/shard_map/ppermute | solution.py:20
  69.7 13.9 %collective-permute-start.5 = (bf16[64,2048]{1,0:T(8,128)(2,1)S(1)}, bf16[64,2048]{1,0:T(8,128)(2,1)S(1)}, u32[]{:S(2)}, u32[]{:S(2)}) collective-permute-start(bf16[64,2048]{1,0:T(8,128)(2,1)S(1)} %collective-permute-done.3), channel_id=1, source_target_pairs={{0,15},{1,0},{2,1},{3,2},{4,3},{5,4},{6,5},{7,6},{8,7},{9,8},{10,9... | collective-permute-start | bytes 786440 | tf_op jit(solution)/shard_map/ppermute | solution.py:23
  73.0 13.7 %collective-permute-start.6 = (bf16[64,2048]{1,0:T(8,128)(2,1)S(1)}, bf16[64,2048]{1,0:T(8,128)(2,1)S(1)}, u32[]{:S(2)}, u32[]{:S(2)}) collective-permute-start(bf16[64,2048]{1,0:T(8,128)(2,1)S(1)} %collective-permute-done.4), channel_id=1, source_target_pairs={{0,1},{1,2},{2,3},{3,4},{4,5},{5,6},{6,7},{7,8},{8,9},{9,10},{10,1... | collective-permute-start | bytes 786440 | tf_op jit(solution)/shard_map/ppermute | solution.py:20
  83.6 13.8 %collective-permute-start.7 = (bf16[64,2048]{1,0:T(8,128)(2,1)S(1)}, bf16[64,2048]{1,0:T(8,128)(2,1)S(1)}, u32[]{:S(2)}, u32[]{:S(2)}) collective-permute-start(bf16[64,2048]{1,0:T(8,128)(2,1)S(1)} %collective-permute-done.5), channel_id=1, source_target_pairs={{0,15},{1,0},{2,1},{3,2},{4,3},{5,4},{6,5},{7,6},{8,7},{9,8},{10,9... | collective-permute-start | bytes 786440 | tf_op jit(solution)/shard_map/ppermute | solution.py:23
  86.8 12.1 %collective-permute-start.8 = (bf16[64,2048]{1,0:T(8,128)(2,1)S(1)}, bf16[64,2048]{1,0:T(8,128)(2,1)S(1)}, u32[]{:S(2)}, u32[]{:S(2)}) collective-permute-start(bf16[64,2048]{1,0:T(8,128)(2,1)S(1)} %collective-permute-done.6), channel_id=1, source_target_pairs={{0,1},{1,2},{2,3},{3,4},{4,5},{5,6},{6,7},{7,8},{8,9},{9,10},{10,1... | collective-permute-start | bytes 786440 | tf_op jit(solution)/shard_map/ppermute | solution.py:20
  97.4 11.3 %collective-permute-start.9 = (bf16[64,2048]{1,0:T(8,128)(2,1)S(1)}, bf16[64,2048]{1,0:T(8,128)(2,1)S(1)}, u32[]{:S(2)}, u32[]{:S(2)}) collective-permute-start(bf16[64,2048]{1,0:T(8,128)(2,1)S(1)} %collective-permute-done.7), channel_id=1, source_target_pairs={{0,15},{1,0},{2,1},{3,2},{4,3},{5,4},{6,5},{7,6},{8,7},{9,8},{10,9... | collective-permute-start | bytes 786440 | tf_op jit(solution)/shard_map/ppermute | solution.py:23
  98.9 13.3 %collective-permute-start.10 = (bf16[64,2048]{1,0:T(8,128)(2,1)S(1)}, bf16[64,2048]{1,0:T(8,128)(2,1)S(1)}, u32[]{:S(2)}, u32[]{:S(2)}) collective-permute-start(bf16[64,2048]{1,0:T(8,128)(2,1)S(1)} %collective-permute-done.8), channel_id=1, source_target_pairs={{0,1},{1,2},{2,3},{3,4},{4,5},{5,6},{6,7},{7,8},{8,9},{9,10},{10,1... | collective-permute-start | bytes 786440 | tf_op jit(solution)/shard_map/ppermute | solution.py:20
  108.8 14.3 %collective-permute-start.11 = (bf16[64,2048]{1,0:T(8,128)(2,1)S(1)}, bf16[64,2048]{1,0:T(8,128)(2,1)S(1)}, u32[]{:S(2)}, u32[]{:S(2)}) collective-permute-start(bf16[64,2048]{1,0:T(8,128)(2,1)S(1)} %collective-permute-done.9), channel_id=1, source_target_pairs={{0,15},{1,0},{2,1},{3,2},{4,3},{5,4},{6,5},{7,6},{8,7},{9,8},{10,9... | collective-permute-start | bytes 786440 | tf_op jit(solution)/shard_map/ppermute | solution.py:23
  112.2 14.2 %collective-permute-start.12 = (bf16[64,2048]{1,0:T(8,128)(2,1)S(1)}, bf16[64,2048]{1,0:T(8,128)(2,1)S(1)}, u32[]{:S(2)}, u32[]{:S(2)}) collective-permute-start(bf16[64,2048]{1,0:T(8,128)(2,1)S(1)} %collective-permute-done.10), channel_id=1, source_target_pairs={{0,1},{1,2},{2,3},{3,4},{4,5},{5,6},{6,7},{7,8},{8,9},{9,10},{10,1... | collective-permute-start | bytes 786440 | tf_op jit(solution)/shard_map/ppermute | solution.py:20
  123.1 9.3 %collective-permute-start.13 = (bf16[64,2048]{1,0:T(8,128)(2,1)S(1)}, bf16[64,2048]{1,0:T(8,128)(2,1)S(1)}, u32[]{:S(2)}, u32[]{:S(2)}) collective-permute-start(bf16[64,2048]{1,0:T(8,128)(2,1)S(1)} %collective-permute-done.11), channel_id=1, source_target_pairs={{0,15},{1,0},{2,1},{3,2},{4,3},{5,4},{6,5},{7,6},{8,7},{9,8},{10,9... | collective-permute-start | bytes 786440 | tf_op jit(solution)/shard_map/ppermute | solution.py:23
  126.5 8.5 %collective-permute-start.14 = (bf16[64,2048]{1,0:T(8,128)(2,1)S(1)}, bf16[64,2048]{1,0:T(8,128)(2,1)S(1)}, u32[]{:S(2)}, u32[]{:S(2)}) collective-permute-start(bf16[64,2048]{1,0:T(8,128)(2,1)S(1)} %collective-permute-done.12), channel_id=1, source_target_pairs={{0,1},{1,2},{2,3},{3,4},{4,5},{5,6},{6,7},{7,8},{8,9},{9,10},{10,1... | collective-permute-start | bytes 786440 | tf_op jit(solution)/shard_map/ppermute | solution.py:20
  135.7 17.8 %copy-start.5 = (f32[8,128]{1,0:T(8,128)S(1)}, f32[8,128]{1,0:T(8,128)}, u32[]{:S(2)}) copy-start(f32[8,128]{1,0:T(8,128)} %param.16) | copy-start | bytes 12292
  135.7 17.8 %copy-start.6 = (f32[8]{0:T(128)S(1)}, f32[8]{0:T(128)}, u32[]{:S(2)}) copy-start(f32[8]{0:T(128)} %param.17) | copy-start | bytes 100
  168.2 4.3 %copy-start.2 = (f32[8,128,128]{1,2,0:T(8,128)S(1)}, f32[8,128,128]{1,2,0:T(8,128)}, u32[]{:S(2)}) copy-start(f32[8,128,128]{1,2,0:T(8,128)} %copy.214) | copy-start | bytes 1572868
  182.9 19.2 %copy-start.1 = (f32[128,1024]{0,1:T(8,128)S(1)}, f32[128,1024]{0,1:T(8,128)}, u32[]{:S(2)}) copy-start(f32[128,1024]{0,1:T(8,128)} %copy-done) | copy-start | bytes 1572868
  (1 other events, 2.2 us)
Sparse Core Ops, SparseCore 0:
  12.8 49.5 all-gather.6
  64.6 86.9 all-gather.8
